TPU v7x, 32 devices: a whole 2x2x4 slice. The times are simulated.
32 devices in a mesh: ri: 2 (over y), mu: 4 (over x, core), nu: 4 (over z).
Axes of the slice: x: 2, y: 2, z: 4, core: 2. Of those that a mesh axis runs over, the one named last changes fastest.
Arguments:
- three_center: bfloat16 [8, 2304, 128, 128], P('ri', ('mu', 'nu')), may hold values from -0.15625 to 0.15625
- block_pairs: int32 [2304, 2], P(('mu', 'nu')), may hold values from -1 to 95, as said below
- occ_factor: bfloat16 [12288, 128], P(('mu', 'nu')), may hold values from -6 to 6
- virt_density: bfloat16 [12288, 12288], P(('mu', 'nu'), 'ri'), may hold values from -0.0546875 to 0.0546875
- block_sizes: int32 [96], replicated, may hold values from 96 to 128
- occ_mask: int32 [96], replicated, may hold values 0 or 1
- virt_mask: int32 [96, 96], replicated, may hold values 0 or 1
Outputs:
- transformed: bfloat16 [8, 12288, 128], P('ri', ('mu', 'nu'))
Inputs may be any that keep to these rules, and one draw needn't show every extreme that they name: `block_pairs`: slots k in [d * 144, (d + 1) * 144) belong to device d of mu+nu; a live slot holds a mu block of that device's mu range (the range of 24 blocks of its mu index) and any nu block; empty slots hold -1 in both columns, and the live slots of a device come first. Every mu block appears in exactly 12 live slots, with distinct nu blocks. A device holds at most 144 live slots, and in every mu range some device holds exactly 144.
All inputs are finite; a program needn't handle non-finite values.
Results may differ from a plain program's by a relative error of at most 0.015.
Values may be sent and summed in bfloat16 or wider, within the bound.
No kernel may reach another device: no remote copies, remote signals or barrier semaphores. Data moves between devices by JAX's collectives and lax.ppermute only.
A program may use at most 192 MiB of HBM per device.

v0:
```python
import jax
import jax.numpy as jnp
from jax import lax
from jax.sharding import PartitionSpec as P

BS = 128
NB = 96


def body(three_center, block_pairs, occ_factor, virt_density, block_sizes, occ_mask, virt_mask):
    rows_dev = virt_density.shape[0]
    occ_cols = occ_factor.shape[1]
    ri_rows = three_center.shape[0]
    blocks_mu = NB // lax.axis_size("mu")
    total_rows = NB * BS
    inside = jnp.arange(BS, dtype=jnp.int32)[None, :] < block_sizes[:, None]
    keep_occ = (inside & (occ_mask[:, None] > 0)).reshape(total_rows)
    gathered_occ = lax.all_gather(occ_factor, ("mu", "nu"), axis=0, tiled=True)
    occ_kept = jnp.where(keep_occ[:, None], gathered_occ, jnp.zeros((), jnp.bfloat16))
    mu_block = block_pairs[:, 0]
    nu_block = jnp.clip(block_pairs[:, 1], 0, NB - 1)
    slot_live = mu_block >= 0
    occ_blocks = occ_kept.reshape(NB, BS, occ_cols)[nu_block]
    products = jnp.einsum(
        "pkab,kbo->pkao", three_center, occ_blocks, preferred_element_type=jnp.float32
    )
    local_block = mu_block - lax.axis_index("mu") * blocks_mu
    segment_ids = jnp.where(slot_live, local_block, blocks_mu)

    def slot_sum(slab_products):
        return jax.ops.segment_sum(slab_products, segment_ids, num_segments=blocks_mu + 1)[
            :blocks_mu
        ]

    partial_value = jax.vmap(slot_sum)(products)
    partial_value = partial_value.reshape(ri_rows, blocks_mu * BS, occ_cols)
    virt_all = lax.all_gather(virt_density, "ri", axis=1, tiled=True)
    row_start = (lax.axis_index("mu") * lax.axis_size("nu") + lax.axis_index("nu")) * rows_dev
    row_ids = row_start + jnp.arange(rows_dev, dtype=jnp.int32)
    block_pick = (row_ids[:, None] // BS == jnp.arange(NB, dtype=jnp.int32)[None, :]).astype(
        jnp.float32
    )
    mask_rows = jnp.dot(block_pick, virt_mask.astype(jnp.float32)) > 0.5
    row_inside = lax.dynamic_slice_in_dim(inside.reshape(total_rows), row_start, rows_dev)
    keep_virt = (mask_rows[:, :, None] & inside[None, :, :] & row_inside[:, None, None]).reshape(
        rows_dev, total_rows
    )
    virt_kept = jnp.where(keep_virt, virt_all, jnp.zeros((), jnp.bfloat16))
    summed = lax.psum(partial_value.astype(jnp.bfloat16), "nu")
    result = jnp.einsum(
        "sm,pmo->pso",
        virt_kept,
        lax.all_gather(summed, "mu", axis=1, tiled=True),
        preferred_element_type=jnp.float32,
    )
    return result.astype(jnp.bfloat16)


def solution(mesh):
    in_specs = (
        P("ri", ("mu", "nu"), None, None),
        P(("mu", "nu"), None),
        P(("mu", "nu"), None),
        P(("mu", "nu"), "ri"),
        P(),
        P(),
        P(),
    )
    out_specs = P("ri", ("mu", "nu"), None)
    return jax.shard_map(body, mesh=mesh, in_specs=in_specs, out_specs=out_specs, check_vma=False)
```

profile of v0, /device:TPU:0, one launch (start us, length us, event | category | flops | bytes accessed | tf_op | source)
XLA Modules:
  0.0 576.3 jit_solution(4603569849631304014)
XLA Ops:
  7.4 0.0 all-gather.4.cloned.1.call-start
  7.4 0.7 all-gather.4.cloned.1.call-update
  8.1 0.0 all-reduce.2.cloned.1.call-start
  8.1 0.8 compare_select_fusion
  8.9 0.7 broadcast_compare_fusion
  9.6 0.7 bitcast_compare_fusion
  10.3 48.4 %all-gather.4.cloned.1.call-done = bf16[12288,128]{1,0:T(8,128)(2,1)} async-done(((bf16[768,128]{1,0:T(8,128)(2,1)}), bf16[12288,128]{1,0:T(8,128)(2,1)}) %all-gather.4.cloned.1.call-update) | async-done | bytes 3145744 | tf_op jit(solution)/shard_map/all_gather | solution.py:18
  58.7 8.4 %broadcast_select_fusion = bf16[12288,128]{1,0:T(8,128)(2,1)S(1)} fusion(bf16[12288,128]{1,0:T(8,128)(2,1)} %all-gather.4.cloned.1.call-done, pred[12288]{0:T(1024)(128)(4,1)S(1)} %get-tuple-element.8), kind=kLoop, calls=%fused_computation.15 | loop fusion | flops 1572864 | bytes 6303744 | tf_op jit(solution)/shard_map/jit(_where)/select_n | solution.py:19
  67.1 7.5 %gather_fusion = bf16[144,128,128]{2,1,0:T(8,128)(2,1)} fusion(bf16[96,128,128]{2,1,0:T(8,128)(2,1)S(1)} %bitcast.47, s32[1024]{0:T(1024)S(1)} %pad_clamp_fusion), kind=kCustom, calls=%fused_computation | custom fusion | bytes 9437760 | tf_op jit(solution)/shard_map/gather | solution.py:23
  74.7 20.3 %fusion.9 = f32[144,4,128,128]{2,3,1,0:T(8,128)} fusion(bf16[4,144,128,128]{3,2,1,0:T(8,128)(2,1)} %param.7, bf16[144,128,128]{2,1,0:T(8,128)(2,1)} %gather_fusion), kind=kOutput, calls=%fused_computation.11 | convolution fusion | flops 2415919104 | bytes 61341696 | tf_op jit(solution)/shard_map/pkab,kbo->pkao/dot_general | solution.py:24
  95.0 36.8 %copy.13 = f32[144,4,128,128]{3,2,1,0:T(8,128)} copy(f32[144,4,128,128]{2,3,1,0:T(8,128)} %fusion.9) | data formatting | bytes 75497472 | tf_op jit(solution)/shard_map/pkab,kbo->pkao/transpose | solution.py:24
  131.8 3.5 broadcast_in_dim.21
  135.3 80.8 %scatter_fusion = f32[4,25,128,128]{3,2,1,0:T(8,128)} fusion(f32[4,25,128,128]{3,2,1,0:T(8,128)} %broadcast_in_dim.21, s32[144]{0:T(256)S(1)} %bitcast.52, f32[144,4,128,128]{3,2,1,0:T(8,128)} %copy.13), kind=kCustom, calls=%fused_computation.1 | custom fusion | flops 9437184 | bytes 113246784 | tf_op jit(solution)/shard_map/vmap()/scatter-add | solution.py:31
  216.1 3.5 slice.19
  219.6 2.8 copy.20
  222.4 0.0 copy-start.1
  222.4 0.0 copy-start
  222.4 0.0 all-reduce.2.cloned.1.call-update
  222.4 0.0 all-gather.8.cloned.1.call-start
  222.5 0.5 all-gather.8.cloned.1.call-update
  223.0 0.2 all-gather.6.cloned.1.call-start
  223.2 120.3 %all-reduce.2.cloned.1.call-done = bf16[4,3072,128]{1,2,0:T(8,128)(2,1)} async-done(((bf16[4,3072,128]{1,2,0:T(8,128)(2,1)}), bf16[4,3072,128]{1,2,0:T(8,128)(2,1)}) %all-reduce.2.cloned.1.call-update) | async-done | bytes 3145744 | tf_op jit(solution)/shard_map/psum | solution.py:49
  343.5 0.0 all-gather.6.cloned.1.call-update
  343.5 0.0 copy-done.1
  343.5 0.3 convolution_compare_fusion
  343.9 0.2 copy.15
  344.1 0.1 dynamic_slice.3
  344.2 0.0 copy-done
  344.2 0.2 lt.49
  344.4 104.0 %all-gather.8.cloned.1.call-done = bf16[768,12288]{1,0:T(8,128)(2,1)} async-done(((bf16[768,6144]{1,0:T(8,128)(2,1)}), bf16[768,12288]{1,0:T(8,128)(2,1)}) %all-gather.8.cloned.1.call-update) | async-done | bytes 18874384 | tf_op jit(solution)/shard_map/all_gather | solution.py:37
  448.4 83.4 %all-gather.6.cloned.1.call-done = bf16[4,12288,128]{1,2,0:T(8,128)(2,1)} async-done(((bf16[4,3072,128]{1,2,0:T(8,128)(2,1)}), bf16[4,12288,128]{1,2,0:T(8,128)(2,1)}) %all-gather.6.cloned.1.call-update) | async-done | bytes 12582928 | tf_op jit(solution)/shard_map/all_gather | solution.py:53
  531.8 13.5 %and.60 = pred[768,96,128]{2,1,0:T(32,128)(4,1)} broadcast(pred[768,96]{1,0:T(8,128)(4,1)S(1)} %copy.15), dimensions={0,1} | broadcast | bytes 9510912 | tf_op jit(solution)/shard_map/and | solution.py:45
  545.3 22.4 %fusion.17 = bf16[4,768,128]{1,2,0:T(8,128)(2,1)S(1)} fusion(bf16[4,12288,128]{1,2,0:T(8,128)(2,1)} %all-gather.6.cloned.1.call-done, bf16[768,12288]{1,0:T(8,128)(2,1)} %all-gather.8.cloned.1.call-done, pred[96,8,96,128]{3,2,1,0:T(32,128)(4,1)} %bitcast.49, pred[768]{0:T(1024)(128)(4,1)S(1)} %dynamic_slice.3, pred[12288]{0:T(1024)(128)(4,1)S(1)} %bitcast_compare_fusion.1), kind=kOutput, calls=%fused_computation.17 | convolution fusion | flops 9692381184 | bytes 41693952 | tf_op jit(solution)/shard_map/sm,pmo->pso/dot_general | solution.py:50
  567.7 1.2 copy.16
  (3 shorter events, 0.0 us)
Async XLA Ops:
  7.4 51.3 %all-gather.4.cloned.1.call-start = ((), (), s32[]{:S(2)}) async-start(), calls=%async_computation | async-start | bytes 3342336 | tf_op jit(solution)/shard_map/all_gather | solution.py:18
  8.1 335.4 %all-reduce.2.cloned.1.call-start = ((), (), s32[]{:S(2)}) async-start(), calls=%async_computation.1 | async-start | bytes 6291456 | tf_op jit(solution)/shard_map/psum | solution.py:49
  222.4 121.2 %copy-start.1 = (s32[96,96]{1,0:T(8,128)S(1)}, s32[96,96]{1,0:T(8,128)}, u32[]{:S(2)}) copy-start(s32[96,96]{1,0:T(8,128)} %param.13) | copy-start | bytes 110596
  222.4 121.8 %copy-start = (s32[96]{0:T(128)S(1)}, s32[96]{0:T(128)}, u32[]{:S(2)}) copy-start(s32[96]{0:T(128)} %param.11) | copy-start | bytes 1156
  222.4 226.0 %all-gather.8.cloned.1.call-start = ((), (), s32[]{:S(2)}) async-start(), calls=%async_computation.3 | async-start | bytes 28311552 | tf_op jit(solution)/shard_map/all_gather | solution.py:37
  223.0 308.8 %all-gather.6.cloned.1.call-start = ((), (), s32[]{:S(2)}) async-start(), calls=%async_computation.2 | async-start | bytes 15728640 | tf_op jit(solution)/shard_map/all_gather | solution.py:53
Sparse Core Ops, SparseCore 0:
  10.5 48.1 all-gather.3
  222.5 120.9 all-reduce.1
Sparse Core Ops, SparseCore 1:
  224.5 223.9 all-gather.7
  449.9 81.9 all-gather.5
where the time goes:
time: 577 us; the launch traced here: 576 us
  waiting for transfers between devices  357 us (62%)
  other arithmetic  91.5 us (16%)
  local copies, waits for them, and re-layouts  69.3 us (12%)
  matrix products  43 us (7%)
  between operations  14.9 us (3%)
    psum x1, waiting for transfers between devices, body(): summed = lax.psum(partial_value.astype(jnp.bfloat16), 'nu')  120 us
    all_gather x1, waiting for transfers between devices, body(): virt_all = lax.all_gather(virt_density, 'ri', axis=1, tiled=True)  104 us
    all_gather x1, waiting for transfers between devices, body(): lax.all_gather(summed, 'mu', axis=1, tiled=True)  83.4 us
    scatter-add x1, other arithmetic, slot_sum(): jax.ops.segment_sum(slab_products, segment_ids, num_segments=blocks_mu + 1)  80.8 us
    all_gather x1, waiting for transfers between devices, body(): gathered_occ = lax.all_gather(occ_factor, ('mu', 'nu'), axis=0, tiled=True)  48.4 us
    transpose x1, local copies, waits for them, and re-layouts, body(): jnp.einsum('pkab,kbo->pkao', three_center, occ_blocks, preferred_element_...  36.8 us
    dot_general x1, matrix products, body(): jnp.einsum('sm,pmo->pso', virt_kept, lax.all_gather(summed, 'mu', axis=1,...  22.4 us
    dot_general x1, matrix products, body(): jnp.einsum('pkab,kbo->pkao', three_center, occ_blocks, preferred_element_...  20.3 us
  transfers between devices with their start and end apart: 4, of which 4 were waited for; matrix products, arithmetic and copies ran while one was open for 1% of the time, Pallas kernels for 0%

commit v1 on v0

--- a/solution.py
+++ b/solution.py
@@ -5,6 +5,11 @@
 
 BS = 128
 NB = 96
+
+
+def add_all(value, name):
+    pieces = lax.all_gather(value, name)
+    return jnp.sum(pieces, axis=0)
 
 
 def body(three_center, block_pairs, occ_factor, virt_density, block_sizes, occ_mask, virt_mask):
@@ -46,7 +51,7 @@
         rows_dev, total_rows
     )
     virt_kept = jnp.where(keep_virt, virt_all, jnp.zeros((), jnp.bfloat16))
-    summed = lax.psum(partial_value.astype(jnp.bfloat16), "nu")
+    summed = add_all(partial_value.astype(jnp.bfloat16), "nu")
     result = jnp.einsum(
         "sm,pmo->pso",
         virt_kept,

time: 577 us -> 791 us (1.37)
  waiting for transfers between devices: 357 us -> 564 us
    all_gather x0 -> x1, waiting for transfers between devices: none -> 217 us  [add_all(): pieces = lax.all_gather(value, name)]
    psum x1 -> x0, waiting for transfers between devices: 120 us -> none  [body(): summed = lax.psum(partial_value.astype(jnp.bfloat16), 'nu')]
    all_gather x1, waiting for transfers between devices: 104 us -> 213 us  [body(): virt_all = lax.all_gather(virt_density, 'ri', axis=1, tiled=True)]
  transfers between devices with their start and end apart: 4 -> 4, of which waited for: 4 -> 4; matrix products, arithmetic and copies ran while one was open for 1% -> 2% of each run, Pallas kernels for 0% -> 0%
where the time goes in v1:
time: 791 us; the launch traced here: 790 us
  waiting for transfers between devices  564 us (71%)
  other arithmetic  98.4 us (12%)
  local copies, waits for them, and re-layouts  71 us (9%)
  matrix products  43 us (5%)
  between operations  13.2 us (2%)
    all_gather x1, waiting for transfers between devices, add_all(): pieces = lax.all_gather(value, name)  217 us
    all_gather x1, waiting for transfers between devices, body(): virt_all = lax.all_gather(virt_density, 'ri', axis=1, tiled=True)  213 us
    all_gather x1, waiting for transfers between devices, body(): lax.all_gather(summed, 'mu', axis=1, tiled=True)  83.5 us
    scatter-add x1, other arithmetic, slot_sum(): jax.ops.segment_sum(slab_products, segment_ids, num_segments=blocks_mu + 1)  80.8 us
    all_gather x1, waiting for transfers between devices, body(): gathered_occ = lax.all_gather(occ_factor, ('mu', 'nu'), axis=0, tiled=True)  48.4 us
    transpose x1, local copies, waits for them, and re-layouts, body(): jnp.einsum('pkab,kbo->pkao', three_center, occ_blocks, preferred_element_...  36.8 us
    dot_general x1, matrix products, body(): jnp.einsum('sm,pmo->pso', virt_kept, lax.all_gather(summed, 'mu', axis=1,...  22.4 us
    dot_general x1, matrix products, body(): jnp.einsum('pkab,kbo->pkao', three_center, occ_blocks, preferred_element_...  20.3 us
  transfers between devices with their start and end apart: 4, of which 4 were waited for; matrix products, arithmetic and copies ran while one was open for 2% of the time, Pallas kernels for 0%

profile of v1, /device:TPU:0, one launch (start us, length us, event | category | flops | bytes accessed | tf_op | source)
XLA Modules:
  0.0 789.7 jit_solution(10363701335061532664)
XLA Ops:
  6.5 0.0 all-gather.5.cloned.1.call-start
  6.5 0.7 all-gather.5.cloned.1.call-update
  7.3 0.0 all-gather.7.cloned.1.call-start
  7.3 0.8 compare_select_fusion
  8.1 0.7 broadcast_compare_fusion
  8.7 0.7 bitcast_compare_fusion
  9.5 48.4 %all-gather.5.cloned.1.call-done = bf16[12288,128]{1,0:T(8,128)(2,1)} async-done(((bf16[768,128]{1,0:T(8,128)(2,1)}), bf16[12288,128]{1,0:T(8,128)(2,1)}) %all-gather.5.cloned.1.call-update) | async-done | bytes 3145744 | tf_op jit(solution)/shard_map/all_gather | solution.py:23
  57.9 8.4 %broadcast_select_fusion = bf16[12288,128]{1,0:T(8,128)(2,1)S(1)} fusion(bf16[12288,128]{1,0:T(8,128)(2,1)} %all-gather.5.cloned.1.call-done, pred[12288]{0:T(1024)(128)(4,1)S(1)} %get-tuple-element.8), kind=kLoop, calls=%fused_computation.15 | loop fusion | flops 1572864 | bytes 6303744 | tf_op jit(solution)/shard_map/jit(_where)/select_n | solution.py:24
  66.3 7.5 gather_fusion
  73.9 20.3 %fusion.9 = f32[144,4,128,128]{2,3,1,0:T(8,128)} fusion(bf16[4,144,128,128]{3,2,1,0:T(8,128)(2,1)} %param.7, bf16[144,128,128]{2,1,0:T(8,128)(2,1)} %gather_fusion), kind=kOutput, calls=%fused_computation.11 | convolution fusion | flops 2415919104 | bytes 61341696 | tf_op jit(solution)/shard_map/pkab,kbo->pkao/dot_general | solution.py:29
  94.1 36.8 %copy.18 = f32[144,4,128,128]{3,2,1,0:T(8,128)} copy(f32[144,4,128,128]{2,3,1,0:T(8,128)} %fusion.9) | data formatting | bytes 75497472 | tf_op jit(solution)/shard_map/pkab,kbo->pkao/transpose | solution.py:29
  131.0 3.5 broadcast_in_dim.21
  134.5 80.8 %scatter_fusion = f32[4,25,128,128]{3,2,1,0:T(8,128)} fusion(f32[4,25,128,128]{3,2,1,0:T(8,128)} %broadcast_in_dim.21, s32[144]{0:T(256)S(1)} %bitcast.52, f32[144,4,128,128]{3,2,1,0:T(8,128)} %copy.18), kind=kCustom, calls=%fused_computation.1 | custom fusion | flops 9437184 | bytes 113246784 | tf_op jit(solution)/shard_map/vmap()/scatter-add | solution.py:36
  215.3 5.1 slice.19
  220.4 0.0 all-gather.7.cloned.1.call-update
  220.4 0.0 all-gather.11.cloned.1.call-start
  220.5 0.7 all-gather.11.cloned.1.call-update
  221.2 0.0 copy-start.1
  221.2 0.0 copy-start
  221.2 0.2 all-gather.9.cloned.1.call-start
  221.4 217.2 %all-gather.7.cloned.1.call-done = bf16[4,4,3072,128]{3,2,1,0:T(8,128)(2,1)} async-done(((bf16[1,4,3072,128]{3,2,1,0:T(8,128)(2,1)}), bf16[4,4,3072,128]{3,2,1,0:T(8,128)(2,1)}) %all-gather.7.cloned.1.call-update) | async-done | bytes 12582928 | tf_op jit(solution)/shard_map/all_gather | solution.py:11
  438.6 6.9 reduce_sum.12
  445.6 2.8 copy.19
  448.4 0.0 all-gather.9.cloned.1.call-update
  448.5 0.0 copy-done.1
  448.5 0.3 convolution_compare_fusion
  448.8 0.2 copy.20
  449.0 0.1 dynamic_slice.3
  449.1 0.0 copy-done
  449.1 0.2 lt.49
  449.3 213.3 %all-gather.11.cloned.1.call-done = bf16[768,12288]{1,0:T(8,128)(2,1)} async-done(((bf16[768,6144]{1,0:T(8,128)(2,1)}), bf16[768,12288]{1,0:T(8,128)(2,1)}) %all-gather.11.cloned.1.call-update) | async-done | bytes 18874384 | tf_op jit(solution)/shard_map/all_gather | solution.py:42
  662.6 83.5 %all-gather.9.cloned.1.call-done = bf16[4,12288,128]{1,2,0:T(8,128)(2,1)} async-done(((bf16[4,3072,128]{1,2,0:T(8,128)(2,1)}), bf16[4,12288,128]{1,2,0:T(8,128)(2,1)}) %all-gather.9.cloned.1.call-update) | async-done | bytes 12582928 | tf_op jit(solution)/shard_map/all_gather | solution.py:58
  746.2 13.5 %and.60 = pred[768,96,128]{2,1,0:T(32,128)(4,1)} broadcast(pred[768,96]{1,0:T(8,128)(4,1)S(1)} %copy.20), dimensions={0,1} | broadcast | bytes 9510912 | tf_op jit(solution)/shard_map/and | solution.py:50
  759.7 22.4 %fusion.17 = bf16[4,768,128]{1,2,0:T(8,128)(2,1)S(1)} fusion(bf16[4,12288,128]{1,2,0:T(8,128)(2,1)} %all-gather.9.cloned.1.call-done, bf16[768,12288]{1,0:T(8,128)(2,1)} %all-gather.11.cloned.1.call-done, pred[96,8,96,128]{3,2,1,0:T(32,128)(4,1)} %bitcast.49, pred[768]{0:T(1024)(128)(4,1)S(1)} %dynamic_slice.3, pred[12288]{0:T(1024)(128)(4,1)S(1)} %bitcast_compare_fusion.1), kind=kOutput, calls=%fused_computation.17 | convolution fusion | flops 9692381184 | bytes 41693952 | tf_op jit(solution)/shard_map/sm,pmo->pso/dot_general | solution.py:55
  782.1 1.2 copy.21
  (3 shorter events, 0.0 us)
Async XLA Ops:
  6.5 51.3 %all-gather.5.cloned.1.call-start = ((), (), s32[]{:S(2)}) async-start(), calls=%async_computation | async-start | bytes 3342336 | tf_op jit(solution)/shard_map/all_gather | solution.py:23
  7.3 431.4 %all-gather.7.cloned.1.call-start = ((), (), s32[]{:S(2)}) async-start(), calls=%async_computation.1 | async-start | bytes 15728640 | tf_op jit(solution)/shard_map/all_gather | solution.py:11
  220.4 442.2 %all-gather.11.cloned.1.call-start = ((), (), s32[]{:S(2)}) async-start(), calls=%async_computation.3 | async-start | bytes 28311552 | tf_op jit(solution)/shard_map/all_gather | solution.py:42
  221.2 227.3 %copy-start.1 = (s32[96,96]{1,0:T(8,128)S(1)}, s32[96,96]{1,0:T(8,128)}, u32[]{:S(2)}) copy-start(s32[96,96]{1,0:T(8,128)} %param.13) | copy-start | bytes 110596
  221.2 228.0 %copy-start = (s32[96]{0:T(128)S(1)}, s32[96]{0:T(128)}, u32[]{:S(2)}) copy-start(s32[96]{0:T(128)} %param.11) | copy-start | bytes 1156
  221.2 525.0 %all-gather.9.cloned.1.call-start = ((), (), s32[]{:S(2)}) async-start(), calls=%async_computation.2 | async-start | bytes 15728640 | tf_op jit(solution)/shard_map/all_gather | solution.py:58
Sparse Core Ops, SparseCore 0:
  9.6 48.1 all-gather.4
  220.5 218.0 all-gather.6
  440.2 222.3 all-gather.10
  664.0 82.0 all-gather.8
